TPU v7x, 256 devices: a whole 4x4x8 slice. The times are simulated.
256 devices in a mesh: slab: 64 (over y, z, x_lo), ffn: 4 (over x_hi, core).
Axes of the slice: x: 4 (x_hi: 2, x_lo: 2; x = x_hi * 2 + x_lo), y: 4, z: 8, core: 2. Of those that a mesh axis runs over, the one named last changes fastest.
Arguments:
- tokens: bfloat16 [32768, 512], P('slab'), may hold values from -6 to 6
- gain_attn: float32 [512], replicated, may hold values from 0.1 to 1.9
- w_reduce: bfloat16 [4096, 512], replicated, may hold values from -0.09375 to 0.09375
- gain_keys: float32 [512], replicated, may hold values from 0.1 to 1.9
- w_query: bfloat16 [512, 512], P(None, 'ffn'), may hold values from -1.5 to 1.5
- w_key: bfloat16 [512, 512], P(None, 'ffn'), may hold values from -1.5 to 1.5
- w_value: bfloat16 [512, 512], P(None, 'ffn'), may hold values from -0.25 to 0.25
- w_out: bfloat16 [512, 512], P('ffn'), may hold values from -1.796875 to 1.796875
- gain_ffn: float32 [512], replicated, may hold values from 0.1 to 1.9
- w_up: bfloat16 [512, 2048], P(None, 'ffn'), may hold values from -0.25 to 0.25
- w_depth: float32 [27, 2048], P(None, 'ffn'), may hold values from -1.25 to 1.25
- w_down: bfloat16 [2048, 512], P('ffn'), may hold values from -0.125 to 0.125
- grad_out: bfloat16 [32768, 512], P('slab'), may hold values from -0.0625 to 0.0625
Outputs:
- attended: bfloat16 [32768, 512], P('slab')
- grad_up: float32 [512, 2048], P('slab', 'ffn')
- grad_down: float32 [512, 2048], P('slab', 'ffn')
All inputs are finite; a program needn't handle non-finite values.
Results may differ from a plain program's by a relative error of at most 0.024.
The roundings to bfloat16 on the way count: a program that leaves them out, or rounds other values in their place, can miss the bound.
Values may be sent and summed in bfloat16 or wider, within the bound.
A program may use at most 64 MiB of HBM per device.

v0:
```python
import math
import jax
import jax.numpy as jnp
from jax import lax
from jax.sharding import Mesh
from jax.sharding import PartitionSpec as P

HEAD = 64
GX = 16
GY = 16
CZ = 2
SLAB = ("y", "z", "xl")
FFN = ("xh", "core")
EPSILON = 1e-05
ROPE_BASE = 100.0
ROOT_HALF = 0.7071067811865476
NORMAL_SCALE = 0.3989422804014327


def padded_2(cells, sides, width):
    for axis, dim in sides:
        count = lax.psum(1, axis)
        ends = count - 1
        head = lax.slice_in_dim(cells, 0, width, axis=dim)
        tail = lax.slice_in_dim(cells, cells.shape[dim] - width, cells.shape[dim], axis=dim)
        cells = jnp.concatenate(
            [
                lax.ppermute(tail, axis, [(i, (i + 1) % count) for i in range(ends)]),
                cells,
                lax.ppermute(head, axis, [((i + 1) % count, i) for i in range(ends)]),
            ],
            axis=dim,
        )
    return cells


def layer_norm(values, scale_gain):
    values = values.astype(jnp.float32)
    centered = values - jnp.mean(values, axis=-1, keepdims=True)
    variance = jnp.mean(centered * centered, axis=-1, keepdims=True)
    return centered * lax.rsqrt(variance + EPSILON) * scale_gain


def rope_tables(coord_x, coord_y, coord_z, head_size):
    pair_count = head_size // 2
    position = jnp.arange(pair_count, dtype=jnp.int32)
    axis_pick = position % 3
    per_axis = (pair_count + 2) // 3
    frequency = ROPE_BASE ** (-(position // 3).astype(jnp.float32) / per_axis)
    angles = (
        coord_x[:, None] * (axis_pick == 0)
        + coord_y[:, None] * (axis_pick == 1)
        + coord_z[:, None] * (axis_pick == 2)
    ) * frequency
    return (jnp.cos(angles)[:, None, :], jnp.sin(angles)[:, None, :])


def token_tables(first_plane, planes, head_size):
    position = jnp.arange(planes * GY * GX, dtype=jnp.int32)
    coord_x = (position % GX).astype(jnp.float32)
    coord_y = (position // GX % GY).astype(jnp.float32)
    coord_z = (first_plane + position // (GX * GY)).astype(jnp.float32)
    return rope_tables(coord_x, coord_y, coord_z, head_size)


def key_tables(first_row, row_count, head_size):
    position = first_row + jnp.arange(row_count, dtype=jnp.int32)
    half_x = GX // 2
    half_y = GY // 2
    coord_x = (position % half_x).astype(jnp.float32) * 2.0 + 0.5
    coord_y = (position // half_x % half_y).astype(jnp.float32) * 2.0 + 0.5
    coord_z = (position // (half_x * half_y)).astype(jnp.float32) * 2.0 + 0.5
    return rope_tables(coord_x, coord_y, coord_z, head_size)


def rotate(values, cosine, sine_table):
    half_size = values.shape[-1] // 2
    front_half = values[..., :half_size]
    back_half = values[..., half_size:]
    return jnp.concatenate(
        [
            front_half * cosine - back_half * sine_table,
            back_half * cosine + front_half * sine_table,
        ],
        axis=-1,
    )


def make_patches(normed, planes):
    width = normed.shape[-1]
    cell_grid = normed.reshape(planes // 2, 2, GY // 2, 2, GX // 2, 2, width)
    return cell_grid.transpose(0, 2, 4, 1, 3, 5, 6).reshape(-1, 8 * width)


def depth_conv(padded, weights, planes):
    height = padded.shape[1] - 2
    width_x = padded.shape[2] - 2
    result = jnp.zeros((planes, height, width_x, padded.shape[3]), jnp.float32)
    for offset in range(27):
        shift_z = offset // 9
        shift_y = offset // 3 % 3
        shift_x = offset % 3
        window = padded[
            shift_z : shift_z + planes, shift_y : shift_y + height, shift_x : shift_x + width_x
        ]
        result = result + window.astype(jnp.float32) * weights[offset]
    return result


def attend_piece(state_tuple, queries, key_rows, value_rows):
    row_max, row_sum, weighted = state_tuple
    score_scale = key_rows.shape[-1] ** (-0.5)
    scores = (
        jnp.einsum("qhd,khd->hqk", queries, key_rows, preferred_element_type=jnp.float32)
        * score_scale
    )
    new_max = jnp.maximum(row_max, jnp.max(scores, axis=2))
    rescale = jnp.exp(row_max - new_max)
    expo = jnp.exp(scores - new_max[:, :, None])
    row_sum = row_sum * rescale + jnp.sum(expo, axis=2)
    weighted = weighted * rescale[:, :, None] + jnp.einsum(
        "hqk,khd->hqd", expo.astype(jnp.bfloat16), value_rows, preferred_element_type=jnp.float32
    )
    return (new_max, row_sum, weighted)


def per_device(
    tokens,
    gain_attn,
    w_reduce,
    gain_keys,
    w_query,
    w_key,
    w_value,
    w_out,
    gain_ffn,
    w_up,
    w_depth,
    w_down,
    grad_out,
):
    slab_index = lax.axis_index(SLAB)
    tok_rows = tokens.shape[0]
    heads_dev = w_query.shape[1] // HEAD
    normed = layer_norm(tokens, gain_attn).astype(jnp.bfloat16)
    patches = make_patches(normed, CZ)
    reduced = jnp.dot(patches, w_reduce, preferred_element_type=jnp.float32)
    key_input = layer_norm(reduced, gain_keys).astype(jnp.bfloat16)
    tok_cos, tok_sin = token_tables(slab_index * CZ, CZ, HEAD)
    queries = jnp.dot(normed, w_query, preferred_element_type=jnp.float32).reshape(
        tok_rows, heads_dev, HEAD
    )
    queries = rotate(queries, tok_cos, tok_sin).astype(jnp.bfloat16)
    initial = (
        jnp.full((heads_dev, tok_rows), -1e30, jnp.float32),
        jnp.zeros((heads_dev, tok_rows), jnp.float32),
        jnp.zeros((heads_dev, tok_rows, HEAD), jnp.float32),
    )
    state_tuple = initial
    local_rows = key_input.shape[0]
    own_cos, own_sin = key_tables(slab_index * local_rows, local_rows, HEAD)
    own_keys = jnp.dot(key_input, w_key, preferred_element_type=jnp.float32).reshape(
        local_rows, heads_dev, HEAD
    )
    own_keys = rotate(own_keys, own_cos, own_sin).astype(jnp.bfloat16)
    own_values = jnp.dot(key_input, w_value, preferred_element_type=jnp.float32).astype(
        jnp.bfloat16
    )
    key_width = heads_dev * HEAD
    pieces = jnp.concatenate([own_keys.reshape(local_rows, key_width), own_values], axis=1)
    for axis in ("xl", "z", "y"):
        pieces = lax.all_gather(pieces, axis, axis=0, tiled=True)
    row_count = pieces.shape[0]
    block_rows = math.gcd(row_count, 1024)
    block_count = row_count // block_rows
    blocks = pieces.reshape(block_count, block_rows, pieces.shape[1])

    def one_block(state_inner, rows_in):
        key_block = rows_in[:, :key_width].reshape(block_rows, heads_dev, HEAD)
        value_block = rows_in[:, key_width:].reshape(block_rows, heads_dev, HEAD)
        return (attend_piece(state_inner, queries, key_block, value_block), None)

    state_tuple, _ = lax.scan(one_block, state_tuple, blocks)
    row_max, row_sum, weighted = state_tuple
    heads_out = (
        (weighted / row_sum[:, :, None])
        .transpose(1, 0, 2)
        .reshape(tok_rows, heads_dev * HEAD)
        .astype(jnp.bfloat16)
    )
    partial_value = jnp.dot(heads_out, w_out, preferred_element_type=jnp.float32)
    head_total = lax.psum(partial_value.astype(jnp.bfloat16), FFN).astype(jnp.float32)
    attended = head_total.astype(jnp.bfloat16)
    residual = tokens.astype(jnp.float32) + head_total
    normed_ffn = layer_norm(residual, gain_ffn).astype(jnp.bfloat16)
    channels = w_up.shape[1]
    pre = (
        jnp.dot(normed_ffn, w_up, preferred_element_type=jnp.float32)
        .astype(jnp.bfloat16)
        .reshape(CZ, GY, GX, channels)
    )
    pre_wide = padded_2(pre, ((SLAB, 0),), 1)
    pre_pad = jnp.pad(pre_wide, ((0, 0), (1, 1), (1, 1), (0, 0)))
    mixed = depth_conv(pre_pad, w_depth, CZ).reshape(tok_rows, channels)
    normal_cdf = 0.5 * (1.0 + lax.erf(mixed * ROOT_HALF))
    normal_pdf = jnp.exp(-0.5 * mixed * mixed) * NORMAL_SCALE
    activated = (mixed * normal_cdf).astype(jnp.bfloat16)
    grad_act = jnp.einsum("td,cd->tc", grad_out, w_down, preferred_element_type=jnp.float32)
    grad_mixed = (
        (grad_act * (normal_cdf + mixed * normal_pdf))
        .astype(jnp.bfloat16)
        .reshape(CZ, GY, GX, channels)
    )
    grad_wide = padded_2(grad_mixed, ((SLAB, 0),), 1)
    grad_pad = jnp.pad(grad_wide, ((0, 0), (1, 1), (1, 1), (0, 0)))
    grad_pre = (
        depth_conv(grad_pad, w_depth[::-1], CZ).astype(jnp.bfloat16).reshape(tok_rows, channels)
    )
    up_full = jnp.einsum("td,tc->dc", normed_ffn, grad_pre, preferred_element_type=jnp.float32)
    down_full = jnp.einsum("td,tc->dc", grad_out, activated, preferred_element_type=jnp.float32)
    grads = jnp.concatenate([up_full, down_full], axis=1)
    sizes = [lax.psum(1, axis) for axis in SLAB]
    grads = grads.reshape(sizes + [-1, grads.shape[1]])
    grads = grads.transpose(1, 0, 2, 3, 4).reshape(-1, grads.shape[-1])
    for axis in ("z", "y", "xl"):
        grads = lax.psum_scatter(grads, axis, scatter_dimension=0, tiled=True)
    return (attended, grads[:, :channels], grads[:, channels:])


def solution(mesh):
    mesh = Mesh(mesh.devices.reshape(4, 8, 2, 2, 2), SLAB + FFN)
    in_specs = (
        P(SLAB, None),
        P(),
        P(),
        P(),
        P(None, FFN),
        P(None, FFN),
        P(None, FFN),
        P(FFN, None),
        P(),
        P(None, FFN),
        P(None, FFN),
        P(FFN, None),
        P(SLAB, None),
    )
    out_specs = (P(SLAB, None), P(SLAB, FFN), P(SLAB, FFN))
    return jax.shard_map(
        per_device, mesh=mesh, in_specs=in_specs, out_specs=out_specs, check_vma=False
    )
```

profile of v0, /device:TPU:1, one launch (start us, length us, event | category | flops | bytes accessed | tf_op | source)
XLA Modules:
  0.0 315.7 jit_solution(17436997218391451417)
XLA Ops:
  7.6 1.2 convert_reduce_fusion
  8.9 1.3 fusion.25
  10.2 1.3 fusion.27
  11.7 0.4 copy.38
  12.1 0.4 reshape.621
  12.5 3.2 %fusion.75 = (f32[64]{0:T(128)S(1)}, f32[64,512]{1,0:T(8,128)S(1)}) fusion(bf16[64,4096]{1,0:T(8,128)(2,1)S(1)} %reshape.621, bf16[4096,512]{1,0:T(8,128)(2,1)} %param.17), kind=kOutput, calls=%fused_computation.155 | convolution fusion | flops 268468160 | bytes 4849920 | tf_op jit(solution)/shard_map/dot_general | solution.py:147
  16.9 4.0 %all_gather.9 = bf16[128,256]{1,0:T(8,128)(2,1)S(1)} all-gather(bf16[64,256]{1,0:T(8,128)(2,1)S(1)} %pad_maximum_fusion.7), channel_id=1, replica_groups=mesh['y'=4,'z'=8,'xl'=2,'xh'=2,'core'=2] {'xl'}, dimensions={0}, use_global_device_ids=true | all-gather | bytes 98304 | tf_op jit(solution)/shard_map/all_gather | solution.py:172
  20.9 25.7 %all_gather.10 = bf16[1024,256]{1,0:T(8,128)(2,1)} all-gather(bf16[128,256]{1,0:T(8,128)(2,1)S(1)} %all_gather.9), channel_id=1, replica_groups=mesh['y'=4,'z'=8,'xl'=2,'xh'=2,'core'=2] {'z'}, dimensions={0}, use_global_device_ids=true | all-gather | bytes 589824 | tf_op jit(solution)/shard_map/all_gather | solution.py:172
  46.7 0.3 fusion.39
  47.0 0.3 fusion.76
  47.4 39.0 %all-gather.2.cloned.1.call-done = bf16[4096,256]{1,0:T(8,128)(2,1)} async-done(((bf16[1024,256]{1,0:T(8,128)(2,1)}), bf16[4096,256]{1,0:T(8,128)(2,1)}) %all-gather.2.cloned.1.call-update) | async-done | bytes 2097168 | tf_op jit(solution)/shard_map/all_gather | solution.py:172
  86.4 33.6 %while.15 = (s32[]{:T(128)}, f32[2,512]{1,0:T(2,128)S(1)}, f32[2,512]{1,0:T(2,128)S(1)}, f32[2,512,64]{1,2,0:T(8,128)S(1)}, bf16[4,1024,256]{2,1,0:T(8,128)(2,1)...) while((s32[]{:T(128)}, f32[2,512]{1,0:T(2,128)S(1)}, f32[2,512]{1,0:T(2,128)S(1)}, ...), condition=%wide.region_7.8_spmd.clone, body=%wide.region_4.7_spmd.clone.sunk | while | flops 277025792 | bytes 33751168 | solution.py:183
  86.4 1.1 constant_dynamic-slice_fusion.2
  87.5 0.2 copy.40
  87.8 2.7 bitcast_reduce_fusion.2
  90.5 3.0 fusion.109
  93.6 0.4 copy-done.1
  93.9 0.9 fusion.111
  94.8 1.1 constant_dynamic-slice_fusion.2
  95.9 0.2 copy.40
  96.2 2.7 bitcast_reduce_fusion.2
  98.9 3.0 fusion.109
  101.9 0.4 copy-done.1
  102.3 0.9 fusion.111
  103.2 1.1 constant_dynamic-slice_fusion.2
  104.6 2.7 bitcast_reduce_fusion.2
  107.3 3.0 fusion.109
  110.3 0.4 copy-done.1
  110.7 0.9 fusion.111
  111.6 1.1 constant_dynamic-slice_fusion.2
  112.7 0.2 copy.40
  112.9 2.7 bitcast_reduce_fusion.2
  115.7 3.0 fusion.109
  118.7 0.4 copy-done.1
  119.1 0.9 fusion.111
  120.1 1.1 convolution_convert_fusion.1
  121.3 47.8 %all-reduce.4.cloned.1.call-done = bf16[512,512]{1,0:T(8,128)(2,1)} async-done(((bf16[512,512]{1,0:T(8,128)(2,1)}), bf16[512,512]{1,0:T(8,128)(2,1)}) %all-reduce.4.cloned.1.call-update) | async-done | bytes 524304 | tf_op jit(solution)/shard_map/psum | solution.py:192
  169.1 1.3 fusion.37
  170.4 1.3 multiply_reduce_fusion
  171.7 1.6 convolution_convert_fusion
  173.3 2.2 collective-permute-start
  175.6 1.3 collective-permute-start.1
  176.9 4.1 %collective-permute-done = bf16[1,16,16,512]{3,2,1,0:T(8,128)(2,1)S(1)} collective-permute-done((bf16[1,16,16,512]{3,2,1,0:T(8,128)(2,1)S(1)}, bf16[1,16,16,512]{3,2,1,0:T(8,128)(2,1)S(1)}, u32[]{:S(2)}, u32[]{:S(2)}) %collective-permute-start) | collective-permute-done | bytes 262176 | tf_op jit(solution)/shard_map/ppermute | solution.py:28
  181.1 10.8 %collective-permute-done.1 = bf16[1,16,16,512]{3,2,1,0:T(8,128)(2,1)S(1)} collective-permute-done((bf16[1,16,16,512]{3,2,1,0:T(8,128)(2,1)S(1)}, bf16[1,16,16,512]{3,2,1,0:T(8,128)(2,1)S(1)}, u32[]{:S(2)}, u32[]{:S(2)}) %collective-permute-start.1) | collective-permute-done | bytes 262176 | tf_op jit(solution)/shard_map/ppermute | solution.py:30
  191.9 0.8 fusion.21
  192.7 3.8 %multiply_add_fusion = f32[2,16,16,512]{3,2,1,0:T(8,128)S(1)} fusion(bf16[2,16,16,512]{3,2,1,0:T(8,128)(2,1)S(1)} %bitcast.119, bf16[4,18,18,512]{3,2,1,0:T(8,128)(2,1)S(1)} %fusion.21, bf16[1,16,16,512]{3,2,1,0:T(8,128)(2,1)S(1)} %collective-permute-done.1, bf16[1,16,16,512]{3,2,1,0:T(8,128)(2,1)S(1)} %collective-permute-done, f32[512]{0:T(512)S(1)} %bitcast.141, ...), kind=kLoop, calls=%fused_computation.59 | loop fusion | flops 21495808 | bytes 14735360 | tf_op jit(solution)/shard_map/add | solution.py:106
  196.5 0.2 fusion.35
  196.8 0.6 fusion.22
  197.4 1.3 collective-permute-start.2
  198.7 1.5 collective-permute-start.3
  200.2 0.5 convolution_bitcast_fusion
  200.6 8.7 %collective-permute-done.2 = bf16[1,16,16,512]{3,2,1,0:T(8,128)(2,1)S(1)} collective-permute-done((bf16[1,16,16,512]{3,2,1,0:T(8,128)(2,1)S(1)}, bf16[1,16,16,512]{3,2,1,0:T(8,128)(2,1)S(1)}, u32[]{:S(2)}, u32[]{:S(2)}) %collective-permute-start.2) | collective-permute-done | bytes 262176 | tf_op jit(solution)/shard_map/ppermute | solution.py:28
  209.3 4.0 %collective-permute-done.3 = bf16[1,16,16,512]{3,2,1,0:T(8,128)(2,1)S(1)} collective-permute-done((bf16[1,16,16,512]{3,2,1,0:T(8,128)(2,1)S(1)}, bf16[1,16,16,512]{3,2,1,0:T(8,128)(2,1)S(1)}, u32[]{:S(2)}, u32[]{:S(2)}) %collective-permute-start.3) | collective-permute-done | bytes 262176 | tf_op jit(solution)/shard_map/ppermute | solution.py:30
  213.3 0.8 select_maximum_fusion
  214.1 3.8 %add_convert_fusion = bf16[2,16,16,512]{3,2,1,0:T(8,128)(2,1)S(1)} fusion(bf16[2,16,16,512]{3,2,1,0:T(8,128)(2,1)S(1)} %bitcast.115, bf16[4,18,18,512]{3,2,1,0:T(8,128)(2,1)S(1)} %select_maximum_fusion, bf16[1,16,16,512]{3,2,1,0:T(8,128)(2,1)S(1)} %collective-permute-done.3, bf16[1,16,16,512]{3,2,1,0:T(8,128)(2,1)S(1)} %collective-permute-done.2, ...), kind=kLoop, calls=%fused_computation.58 | loop fusion | flops 21757952 | bytes 14211072 | tf_op jit(solution)/shard_map/convert_element_type | solution.py:217
  217.9 0.6 fusion.67
  218.6 0.3 pad_maximum_fusion
  218.9 1.8 copy.33
  220.7 3.2 %copy.34 = f32[8,4,2,8,1024]{4,3,2,1,0:T(8,128)} copy(f32[8,4,2,8,1024]{4,3,2,0,1:T(8,128)} %bitcast.117) | data formatting | bytes 4194304 | tf_op jit(solution)/shard_map/transpose | solution.py:224
  223.9 37.7 %reduce-scatter.4.cloned.1.call-done = f32[64,1024]{1,0:T(8,128)} async-done(((f32[512,1024]{1,0:T(8,128)}), f32[64,1024]{1,0:T(8,128)}) %reduce-scatter.4.cloned.1.call-update) | async-done | bytes 262160 | tf_op jit(solution)/shard_map/reduce_scatter | solution.py:226
  261.7 26.5 %reduce-scatter.6.cloned.1.call-done = f32[16,1024]{1,0:T(8,128)} async-done(((f32[64,1024]{1,0:T(8,128)}), f32[16,1024]{1,0:T(8,128)}) %reduce-scatter.6.cloned.1.call-update) | async-done | bytes 65552 | tf_op jit(solution)/shard_map/reduce_scatter | solution.py:226
  288.2 18.9 %reduce-scatter.8.cloned.1.call-done = f32[8,1024]{1,0:T(8,128)} async-done(((f32[16,1024]{1,0:T(8,128)}), f32[8,1024]{1,0:T(8,128)}) %reduce-scatter.8.cloned.1.call-update) | async-done | bytes 32784 | tf_op jit(solution)/shard_map/reduce_scatter | solution.py:226
  307.1 1.3 fusion.74
  308.4 0.8 copy.54
  (90 shorter events, 2.7 us)
Async XLA Ops:
  7.2 189.6 %copy-start = (bf16[512,512]{1,0:T(8,128)(2,1)S(1)}, bf16[512,512]{1,0:T(8,128)(2,1)}, u32[]{:S(2)}) copy-start(bf16[512,512]{1,0:T(8,128)(2,1)} %param.27) | copy-start | bytes 1572868
  7.2 79.2 %all-gather.2.cloned.1.call-start = ((), (), s32[]{:S(2)}) async-start(), calls=%async_computation.3 | async-start | bytes 2621440 | tf_op jit(solution)/shard_map/all_gather | solution.py:172
  11.7 4.2 %copy-start.6 = (bf16[512,128]{1,0:T(8,128)(2,1)S(1)}, bf16[512,128]{1,0:T(8,128)(2,1)}, u32[]{:S(2)}) copy-start(bf16[512,128]{1,0:T(8,128)(2,1)} %param.20) | copy-start | bytes 393220
  11.7 4.2 %copy-start.10 = (f32[512]{0:T(512)S(1)}, f32[512]{0:T(512)}, u32[]{:S(2)}) copy-start(f32[512]{0:T(512)} %param.18) | copy-start | bytes 6148
  12.1 4.5 %copy-start.7 = (bf16[512,128]{1,0:T(8,128)(2,1)S(1)}, bf16[512,128]{1,0:T(8,128)(2,1)}, u32[]{:S(2)}) copy-start(bf16[512,128]{1,0:T(8,128)(2,1)} %param.21) | copy-start | bytes 393220
  12.5 34.5 %copy-start.5 = (bf16[512,128]{1,0:T(8,128)(2,1)S(1)}, bf16[512,128]{1,0:T(8,128)(2,1)}, u32[]{:S(2)}) copy-start(bf16[512,128]{1,0:T(8,128)(2,1)} %param.19) | copy-start | bytes 393220
  46.6 122.5 %all-reduce.4.cloned.1.call-start = ((), (), s32[]{:S(2)}) async-start(), calls=%async_computation.4 | async-start | bytes 1048576 | tf_op jit(solution)/shard_map/psum | solution.py:192
  86.4 33.7 %copy-start.8 = (bf16[128,512]{1,0:T(8,128)(2,1)S(1)}, bf16[128,512]{1,0:T(8,128)(2,1)}, u32[]{:S(2)}) copy-start(bf16[128,512]{1,0:T(8,128)(2,1)} %param.22) | copy-start | bytes 393220
  86.4 82.7 %copy-start.2 = (bf16[512,512]{1,0:T(8,128)(2,1)S(1)}, bf16[512,512]{1,0:T(8,128)(2,1)}, u32[]{:S(2)}) copy-start(bf16[512,512]{1,0:T(8,128)(2,1)} %param.15) | copy-start | bytes 1572868
  90.5 3.4 %copy-start.1 = (f32[2,1024,512]{2,1,0:T(8,128)S(1)}, f32[2,1024,512]{2,1,0:T(8,128)}, u32[]{:S(2)}) copy-start(f32[2,1024,512]{2,1,0:T(8,128)} %get-tuple-element.197) | copy-start | bytes 12582916 | tf_op jit(solution)/shard_map/while
  98.9 3.4 %copy-start.1 = (f32[2,1024,512]{2,1,0:T(8,128)S(1)}, f32[2,1024,512]{2,1,0:T(8,128)}, u32[]{:S(2)}) copy-start(f32[2,1024,512]{2,1,0:T(8,128)} %get-tuple-element.197) | copy-start | bytes 12582916 | tf_op jit(solution)/shard_map/while
  107.3 3.4 %copy-start.1 = (f32[2,1024,512]{2,1,0:T(8,128)S(1)}, f32[2,1024,512]{2,1,0:T(8,128)}, u32[]{:S(2)}) copy-start(f32[2,1024,512]{2,1,0:T(8,128)} %get-tuple-element.197) | copy-start | bytes 12582916 | tf_op jit(solution)/shard_map/while
  115.6 3.4 %copy-start.1 = (f32[2,1024,512]{2,1,0:T(8,128)S(1)}, f32[2,1024,512]{2,1,0:T(8,128)}, u32[]{:S(2)}) copy-start(f32[2,1024,512]{2,1,0:T(8,128)} %get-tuple-element.197) | copy-start | bytes 12582916 | tf_op jit(solution)/shard_map/while
  120.0 51.7 %copy-start.11 = (bf16[512,512]{1,0:T(8,128)(2,1)S(1)}, bf16[512,512]{1,0:T(8,128)(2,1)}, u32[]{:S(2)}) copy-start(bf16[512,512]{1,0:T(8,128)(2,1)} %param.24) | copy-start | bytes 1572868
  120.0 51.7 %copy-start.12 = (f32[512]{0:T(512)S(1)}, f32[512]{0:T(512)}, u32[]{:S(2)}) copy-start(f32[512]{0:T(512)} %param.23) | copy-start | bytes 6148
  120.1 56.8 %copy-start.9 = (f32[27,512]{1,0:T(8,128)S(1)}, f32[27,512]{1,0:T(8,128)}, u32[]{:S(2)}) copy-start(f32[27,512]{1,0:T(8,128)} %param.25) | copy-start | bytes 165892
  121.2 140.4 %reduce-scatter.4.cloned.1.call-start = ((), (), s32[]{:S(2)}) async-start(), calls=%async_computation.5 | async-start | bytes 2359296 | tf_op jit(solution)/shard_map/reduce_scatter | solution.py:226
  173.3 7.7 %collective-permute-start = (bf16[1,16,16,512]{3,2,1,0:T(8,128)(2,1)S(1)}, bf16[1,16,16,512]{3,2,1,0:T(8,128)(2,1)S(1)}, u32[]{:S(2)}, u32[]{:S(2)}) collective-permute-start(bf16[1,16,16,512]{3,2,1,0:T(8,128)(2,1)S(1)} %bitcast.126), channel_id=1, source_target_pairs={{0,4},{4,8},{8,12},{12,16},{16,20},{20,24},{24,28},{28,32},{32,36}... | collective-permute-start | bytes 786440 | tf_op jit(solution)/shard_map/ppermute | solution.py:28
  175.6 16.3 %collective-permute-start.1 = (bf16[1,16,16,512]{3,2,1,0:T(8,128)(2,1)S(1)}, bf16[1,16,16,512]{3,2,1,0:T(8,128)(2,1)S(1)}, u32[]{:S(2)}, u32[]{:S(2)}) collective-permute-start(bf16[1,16,16,512]{3,2,1,0:T(8,128)(2,1)S(1)} %bitcast.125), channel_id=1, source_target_pairs={{4,0},{8,4},{12,8},{16,12},{20,16},{24,20},{28,24},{32,28},{36,32}... | collective-permute-start | bytes 786440 | tf_op jit(solution)/shard_map/ppermute | solution.py:30
  192.7 4.1 %copy-start.4 = (bf16[512,512]{1,0:T(8,128)(2,1)S(1)}, bf16[512,512]{1,0:T(8,128)(2,1)}, u32[]{:S(2)}) copy-start(bf16[512,512]{1,0:T(8,128)(2,1)} %param.26) | copy-start | bytes 1572868
  197.4 11.9 %collective-permute-start.2 = (bf16[1,16,16,512]{3,2,1,0:T(8,128)(2,1)S(1)}, bf16[1,16,16,512]{3,2,1,0:T(8,128)(2,1)S(1)}, u32[]{:S(2)}, u32[]{:S(2)}) collective-permute-start(bf16[1,16,16,512]{3,2,1,0:T(8,128)(2,1)S(1)} %bitcast.128), channel_id=1, source_target_pairs={{0,4},{4,8},{8,12},{12,16},{16,20},{20,24},{24,28},{28,32},{32,36}... | collective-permute-start | bytes 786440 | tf_op jit(solution)/shard_map/ppermute | solution.py:28
  198.7 14.6 %collective-permute-start.3 = (bf16[1,16,16,512]{3,2,1,0:T(8,128)(2,1)S(1)}, bf16[1,16,16,512]{3,2,1,0:T(8,128)(2,1)S(1)}, u32[]{:S(2)}, u32[]{:S(2)}) collective-permute-start(bf16[1,16,16,512]{3,2,1,0:T(8,128)(2,1)S(1)} %bitcast.127), channel_id=1, source_target_pairs={{4,0},{8,4},{12,8},{16,12},{20,16},{24,20},{28,24},{32,28},{36,32}... | collective-permute-start | bytes 786440 | tf_op jit(solution)/shard_map/ppermute | solution.py:30
  214.1 3.9 %copy-start.3 = (bf16[512,512]{1,0:T(8,128)(2,1)S(1)}, bf16[512,512]{1,0:T(8,128)(2,1)}, u32[]{:S(2)}) copy-start(bf16[512,512]{1,0:T(8,128)(2,1)} %all-reduce.4.cloned.1.call-done) | copy-start | bytes 1572868
  223.9 64.3 %reduce-scatter.6.cloned.1.call-start = ((), (), s32[]{:S(2)}) async-start(), calls=%async_computation.6 | async-start | bytes 327680 | tf_op jit(solution)/shard_map/reduce_scatter | solution.py:226
  261.7 45.4 %reduce-scatter.8.cloned.1.call-start = ((), (), s32[]{:S(2)}) async-start(), calls=%async_computation.7 | async-start | bytes 98304 | tf_op jit(solution)/shard_map/reduce_scatter | solution.py:226
Sparse Core Ops, SparseCore 0:
  46.7 39.6 all-gather.1
  121.3 47.7 all-reduce.3
  224.0 37.5 reduce-scatter.3
  264.0 24.1 reduce-scatter.5
  290.6 16.4 reduce-scatter.7
where the time goes:
time: 316 us
  waiting for transfers between devices  198 us (63%)
  blocking collectives  29.7 us (9%)
  other arithmetic  29.5 us (9%)
  matrix products  22.5 us (7%)
  local copies, waits for them, and re-layouts  15.5 us (5%)
  between operations  14.3 us (5%)
  starting transfers between devices  6.48 us (2%)
    reduce_scatter x3, waiting for transfers between devices, per_device(): grads = lax.psum_scatter(grads, axis, scatter_dimension=0, tiled=True)  83 us
    psum x1, waiting for transfers between devices, per_device(): lax.psum(partial_value.astype(jnp.bfloat16), FFN).astype(jnp.float32)  47.8 us
    all_gather x1, waiting for transfers between devices, per_device(): pieces = lax.all_gather(pieces, axis, axis=0, tiled=True)  39 us
    all_gather x2, blocking collectives, per_device(): pieces = lax.all_gather(pieces, axis, axis=0, tiled=True)  29.7 us
    ppermute x2, waiting for transfers between devices, padded_2(): lax.ppermute(head, axis, [((i + 1) % count, i) for i in range(ends)])  14.8 us
    ppermute x2, waiting for transfers between devices, padded_2(): lax.ppermute(tail, axis, [(i, (i + 1) % count) for i in range(ends)])  12.8 us
    reduce_sum x4, other arithmetic, attend_piece(): row_sum = row_sum * rescale + jnp.sum(expo, axis=2)  12.1 us
    dot_general x4, matrix products, attend_piece(): jnp.einsum('qhd,khd->hqk', queries, key_rows, preferred_element_type=jnp....  10.8 us
  transfers between devices with their start and end apart: 9, of which 9 were waited for; matrix products, arithmetic and copies ran while one was open for 0% of the time, Pallas kernels for 0%

commit v1 on v0

--- a/solution.py
+++ b/solution.py
@@ -189,7 +189,12 @@
         .astype(jnp.bfloat16)
     )
     partial_value = jnp.dot(heads_out, w_out, preferred_element_type=jnp.float32)
-    head_total = lax.psum(partial_value.astype(jnp.bfloat16), FFN).astype(jnp.float32)
+
+    def _return_all_thing(shard_in, mesh_name):
+        x_new = lax.all_gather(shard_in, axis_name=mesh_name)
+        return jnp.sum(x_new, 0)
+
+    head_total = _return_all_thing(partial_value.astype(jnp.bfloat16), FFN).astype(jnp.float32)
     attended = head_total.astype(jnp.bfloat16)
     residual = tokens.astype(jnp.float32) + head_total
     normed_ffn = layer_norm(residual, gain_ffn).astype(jnp.bfloat16)

time: 316 us -> 296 us (0.937)
  waiting for transfers between devices: 198 us -> 179 us
    psum x1 -> x0, waiting for transfers between devices: 47.8 us -> none  [per_device(): lax.psum(partial_value.astype(jnp.bfloat16), FFN).astype(jnp.float32)]
    all_gather x0 -> x1, waiting for transfers between devices: none -> 29.7 us  [_return_all_thing(): x_new = lax.all_gather(shard_in, axis_name=mesh_name)]
where the time goes in v1:
time: 296 us
  waiting for transfers between devices  179 us (60%)
  blocking collectives  29.7 us (10%)
  other arithmetic  29.6 us (10%)
  matrix products  21.5 us (7%)
  local copies, waits for them, and re-layouts  14.7 us (5%)
  between operations  14.3 us (5%)
  starting transfers between devices  6.48 us (2%)
    reduce_scatter x3, waiting for transfers between devices, per_device(): grads = lax.psum_scatter(grads, axis, scatter_dimension=0, tiled=True)  83 us
    all_gather x1, waiting for transfers between devices, per_device(): pieces = lax.all_gather(pieces, axis, axis=0, tiled=True)  39 us
    all_gather x1, waiting for transfers between devices, _return_all_thing(): x_new = lax.all_gather(shard_in, axis_name=mesh_name)  29.7 us
    all_gather x2, blocking collectives, per_device(): pieces = lax.all_gather(pieces, axis, axis=0, tiled=True)  29.7 us
    ppermute x2, waiting for transfers between devices, padded_2(): lax.ppermute(head, axis, [((i + 1) % count, i) for i in range(ends)])  14.9 us
    ppermute x2, waiting for transfers between devices, padded_2(): lax.ppermute(tail, axis, [(i, (i + 1) % count) for i in range(ends)])  12.7 us
    reduce_sum x4, other arithmetic, attend_piece(): row_sum = row_sum * rescale + jnp.sum(expo, axis=2)  12.1 us
    dot_general x4, matrix products, attend_piece(): jnp.einsum('qhd,khd->hqk', queries, key_rows, preferred_element_type=jnp....  10.8 us
  transfers between devices with their start and end apart: 9, of which 9 were waited for; matrix products, arithmetic and copies ran while one was open for 0% of the time, Pallas kernels for 0%

profile of v1, /device:TPU:1, one launch (start us, length us, event | category | flops | bytes accessed | tf_op | source)
XLA Modules:
  0.0 295.8 jit_solution(15401518026993502075)
XLA Ops:
  7.6 1.2 convert_reduce_fusion
  8.9 1.3 fusion.25
  10.2 1.3 fusion.27
  11.7 0.4 copy.38
  12.1 0.4 reshape.621
  12.5 3.2 %fusion.75 = (f32[64]{0:T(128)S(1)}, f32[64,512]{1,0:T(8,128)S(1)}) fusion(bf16[64,4096]{1,0:T(8,128)(2,1)S(1)} %reshape.621, bf16[4096,512]{1,0:T(8,128)(2,1)} %param.17), kind=kOutput, calls=%fused_computation.155 | convolution fusion | flops 268468160 | bytes 4849920 | tf_op jit(solution)/shard_map/dot_general | solution.py:147
  16.9 4.0 %all_gather.15 = bf16[128,256]{1,0:T(8,128)(2,1)S(1)} all-gather(bf16[64,256]{1,0:T(8,128)(2,1)S(1)} %pad_maximum_fusion.7), channel_id=1, replica_groups=mesh['y'=4,'z'=8,'xl'=2,'xh'=2,'core'=2] {'xl'}, dimensions={0}, use_global_device_ids=true | all-gather | bytes 98304 | tf_op jit(solution)/shard_map/all_gather | solution.py:172
  20.9 25.7 %all_gather.16 = bf16[1024,256]{1,0:T(8,128)(2,1)} all-gather(bf16[128,256]{1,0:T(8,128)(2,1)S(1)} %all_gather.15), channel_id=1, replica_groups=mesh['y'=4,'z'=8,'xl'=2,'xh'=2,'core'=2] {'z'}, dimensions={0}, use_global_device_ids=true | all-gather | bytes 589824 | tf_op jit(solution)/shard_map/all_gather | solution.py:172
  46.7 0.3 fusion.39
  47.0 0.3 fusion.76
  47.4 39.0 %all-gather.4.cloned.1.call-done = bf16[4096,256]{1,0:T(8,128)(2,1)} async-done(((bf16[1024,256]{1,0:T(8,128)(2,1)}), bf16[4096,256]{1,0:T(8,128)(2,1)}) %all-gather.4.cloned.1.call-update) | async-done | bytes 2097168 | tf_op jit(solution)/shard_map/all_gather | solution.py:172
  86.4 33.6 %while.15 = (s32[]{:T(128)}, f32[2,512]{1,0:T(2,128)S(1)}, f32[2,512]{1,0:T(2,128)S(1)}, f32[2,512,64]{1,2,0:T(8,128)S(1)}, bf16[4,1024,256]{2,1,0:T(8,128)(2,1)...) while((s32[]{:T(128)}, f32[2,512]{1,0:T(2,128)S(1)}, f32[2,512]{1,0:T(2,128)S(1)}, ...), condition=%wide.region_7.8_spmd.clone, body=%wide.region_4.7_spmd.clone.sunk | while | flops 277025792 | bytes 33751168 | solution.py:183
  86.4 1.1 constant_dynamic-slice_fusion.2
  87.5 0.2 copy.40
  87.7 2.7 bitcast_reduce_fusion.2
  90.5 3.0 %fusion.109 = f32[2,512]{1,0:T(2,128)S(1)} fusion(f32[2,1024,512]{2,1,0:T(8,128)} %get-tuple-element.197, f32[2,512]{1,0:T(2,128)S(1)} %fusion.108), kind=kLoop, calls=%fused_computation.4.clone.1 | loop fusion | flops 3144704 | bytes 4202496 | tf_op jit(solution)/shard_map/while/body/eval_jaxpr/reduce_sum | solution.py:120
  93.5 0.4 copy-done.1
  93.9 0.9 fusion.111
  94.8 1.1 constant_dynamic-slice_fusion.2
  95.9 0.2 copy.40
  96.1 2.7 bitcast_reduce_fusion.2
  98.8 3.0 %fusion.109 = f32[2,512]{1,0:T(2,128)S(1)} fusion(f32[2,1024,512]{2,1,0:T(8,128)} %get-tuple-element.197, f32[2,512]{1,0:T(2,128)S(1)} %fusion.108), kind=kLoop, calls=%fused_computation.4.clone.1 | loop fusion | flops 3144704 | bytes 4202496 | tf_op jit(solution)/shard_map/while/body/eval_jaxpr/reduce_sum | solution.py:120
  101.9 0.4 copy-done.1
  102.3 0.9 fusion.111
  103.2 1.1 constant_dynamic-slice_fusion.2
  104.3 0.2 copy.40
  104.5 2.7 bitcast_reduce_fusion.2
  107.2 3.0 %fusion.109 = f32[2,512]{1,0:T(2,128)S(1)} fusion(f32[2,1024,512]{2,1,0:T(8,128)} %get-tuple-element.197, f32[2,512]{1,0:T(2,128)S(1)} %fusion.108), kind=kLoop, calls=%fused_computation.4.clone.1 | loop fusion | flops 3144704 | bytes 4202496 | tf_op jit(solution)/shard_map/while/body/eval_jaxpr/reduce_sum | solution.py:120
  110.3 0.4 copy-done.1
  110.7 0.9 fusion.111
  111.6 1.1 constant_dynamic-slice_fusion.2
  112.9 2.7 bitcast_reduce_fusion.2
  115.6 3.0 %fusion.109 = f32[2,512]{1,0:T(2,128)S(1)} fusion(f32[2,1024,512]{2,1,0:T(8,128)} %get-tuple-element.197, f32[2,512]{1,0:T(2,128)S(1)} %fusion.108), kind=kLoop, calls=%fused_computation.4.clone.1 | loop fusion | flops 3144704 | bytes 4202496 | tf_op jit(solution)/shard_map/while/body/eval_jaxpr/reduce_sum | solution.py:120
  118.7 0.4 copy-done.1
  119.1 0.9 fusion.111
  120.0 1.1 convolution_convert_fusion.1
  121.2 29.7 %all-gather.6.cloned.1.call-done = bf16[2048,512]{1,0:T(8,128)(2,1)} async-done(((bf16[512,512]{1,0:T(8,128)(2,1)}), bf16[2048,512]{1,0:T(8,128)(2,1)}) %all-gather.6.cloned.1.call-update) | async-done | bytes 2097168 | tf_op jit(solution)/shard_map/all_gather | solution.py:194
  150.9 2.2 reduce_sum.79
  153.1 0.2 fusion.37
  153.4 0.3 multiply_reduce_fusion
  153.7 0.5 convolution_convert_fusion
  154.3 2.2 collective-permute-start
  156.5 1.3 collective-permute-start.1
  157.9 4.0 %collective-permute-done = bf16[1,16,16,512]{3,2,1,0:T(8,128)(2,1)S(1)} collective-permute-done((bf16[1,16,16,512]{3,2,1,0:T(8,128)(2,1)S(1)}, bf16[1,16,16,512]{3,2,1,0:T(8,128)(2,1)S(1)}, u32[]{:S(2)}, u32[]{:S(2)}) %collective-permute-start) | collective-permute-done | bytes 262176 | tf_op jit(solution)/shard_map/ppermute | solution.py:28
  161.9 10.9 %collective-permute-done.1 = bf16[1,16,16,512]{3,2,1,0:T(8,128)(2,1)S(1)} collective-permute-done((bf16[1,16,16,512]{3,2,1,0:T(8,128)(2,1)S(1)}, bf16[1,16,16,512]{3,2,1,0:T(8,128)(2,1)S(1)}, u32[]{:S(2)}, u32[]{:S(2)}) %collective-permute-start.1) | collective-permute-done | bytes 262176 | tf_op jit(solution)/shard_map/ppermute | solution.py:30
  172.8 0.8 fusion.21
  173.6 3.8 %multiply_add_fusion = f32[2,16,16,512]{3,2,1,0:T(8,128)S(1)} fusion(bf16[2,16,16,512]{3,2,1,0:T(8,128)(2,1)S(1)} %bitcast.120, bf16[4,18,18,512]{3,2,1,0:T(8,128)(2,1)S(1)} %fusion.21, bf16[1,16,16,512]{3,2,1,0:T(8,128)(2,1)S(1)} %collective-permute-done.1, bf16[1,16,16,512]{3,2,1,0:T(8,128)(2,1)S(1)} %collective-permute-done, f32[512]{0:T(512)S(1)} %bitcast.143, ...), kind=kLoop, calls=%fused_computation.59 | loop fusion | flops 21495808 | bytes 14735360 | tf_op jit(solution)/shard_map/add | solution.py:106
  177.4 0.2 fusion.35
  177.7 0.6 fusion.22
  178.3 1.3 collective-permute-start.2
  179.6 1.5 collective-permute-start.3
  181.1 0.5 convolution_bitcast_fusion
  181.6 8.7 %collective-permute-done.2 = bf16[1,16,16,512]{3,2,1,0:T(8,128)(2,1)S(1)} collective-permute-done((bf16[1,16,16,512]{3,2,1,0:T(8,128)(2,1)S(1)}, bf16[1,16,16,512]{3,2,1,0:T(8,128)(2,1)S(1)}, u32[]{:S(2)}, u32[]{:S(2)}) %collective-permute-start.2) | collective-permute-done | bytes 262176 | tf_op jit(solution)/shard_map/ppermute | solution.py:28
  190.2 4.0 %collective-permute-done.3 = bf16[1,16,16,512]{3,2,1,0:T(8,128)(2,1)S(1)} collective-permute-done((bf16[1,16,16,512]{3,2,1,0:T(8,128)(2,1)S(1)}, bf16[1,16,16,512]{3,2,1,0:T(8,128)(2,1)S(1)}, u32[]{:S(2)}, u32[]{:S(2)}) %collective-permute-start.3) | collective-permute-done | bytes 262176 | tf_op jit(solution)/shard_map/ppermute | solution.py:30
  194.2 0.8 select_maximum_fusion
  195.0 3.8 %add_convert_fusion = bf16[2,16,16,512]{3,2,1,0:T(8,128)(2,1)S(1)} fusion(bf16[2,16,16,512]{3,2,1,0:T(8,128)(2,1)S(1)} %bitcast.116, bf16[4,18,18,512]{3,2,1,0:T(8,128)(2,1)S(1)} %select_maximum_fusion, bf16[1,16,16,512]{3,2,1,0:T(8,128)(2,1)S(1)} %collective-permute-done.3, bf16[1,16,16,512]{3,2,1,0:T(8,128)(2,1)S(1)} %collective-permute-done.2, ...), kind=kLoop, calls=%fused_computation.58 | loop fusion | flops 21757952 | bytes 14211072 | tf_op jit(solution)/shard_map/convert_element_type | solution.py:222
  198.8 0.7 fusion.67
  199.5 0.3 pad_maximum_fusion
  199.8 1.8 copy.33
  201.6 3.2 %copy.34 = f32[8,4,2,8,1024]{4,3,2,1,0:T(8,128)} copy(f32[8,4,2,8,1024]{4,3,2,0,1:T(8,128)} %bitcast.118) | data formatting | bytes 4194304 | tf_op jit(solution)/shard_map/transpose | solution.py:229
  204.8 37.7 %reduce-scatter.4.cloned.1.call-done = f32[64,1024]{1,0:T(8,128)} async-done(((f32[512,1024]{1,0:T(8,128)}), f32[64,1024]{1,0:T(8,128)}) %reduce-scatter.4.cloned.1.call-update) | async-done | bytes 262160 | tf_op jit(solution)/shard_map/reduce_scatter | solution.py:231
  242.6 26.5 %reduce-scatter.6.cloned.1.call-done = f32[16,1024]{1,0:T(8,128)} async-done(((f32[64,1024]{1,0:T(8,128)}), f32[16,1024]{1,0:T(8,128)}) %reduce-scatter.6.cloned.1.call-update) | async-done | bytes 65552 | tf_op jit(solution)/shard_map/reduce_scatter | solution.py:231
  269.1 18.8 %reduce-scatter.8.cloned.1.call-done = f32[8,1024]{1,0:T(8,128)} async-done(((f32[16,1024]{1,0:T(8,128)}), f32[8,1024]{1,0:T(8,128)}) %reduce-scatter.8.cloned.1.call-update) | async-done | bytes 32784 | tf_op jit(solution)/shard_map/reduce_scatter | solution.py:231
  288.0 1.3 fusion.74
  (90 shorter events, 2.8 us)
Async XLA Ops:
  7.2 170.5 %copy-start = (bf16[512,512]{1,0:T(8,128)(2,1)S(1)}, bf16[512,512]{1,0:T(8,128)(2,1)}, u32[]{:S(2)}) copy-start(bf16[512,512]{1,0:T(8,128)(2,1)} %param.27) | copy-start | bytes 1572868
  7.2 79.2 %all-gather.4.cloned.1.call-start = ((), (), s32[]{:S(2)}) async-start(), calls=%async_computation.3 | async-start | bytes 2621440 | tf_op jit(solution)/shard_map/all_gather | solution.py:172
  11.7 4.2 %copy-start.6 = (bf16[512,128]{1,0:T(8,128)(2,1)S(1)}, bf16[512,128]{1,0:T(8,128)(2,1)}, u32[]{:S(2)}) copy-start(bf16[512,128]{1,0:T(8,128)(2,1)} %param.20) | copy-start | bytes 393220
  11.7 4.2 %copy-start.10 = (f32[512]{0:T(512)S(1)}, f32[512]{0:T(512)}, u32[]{:S(2)}) copy-start(f32[512]{0:T(512)} %param.18) | copy-start | bytes 6148
  12.1 4.5 %copy-start.7 = (bf16[512,128]{1,0:T(8,128)(2,1)S(1)}, bf16[512,128]{1,0:T(8,128)(2,1)}, u32[]{:S(2)}) copy-start(bf16[512,128]{1,0:T(8,128)(2,1)} %param.21) | copy-start | bytes 393220
  12.5 34.5 %copy-start.5 = (bf16[512,128]{1,0:T(8,128)(2,1)S(1)}, bf16[512,128]{1,0:T(8,128)(2,1)}, u32[]{:S(2)}) copy-start(bf16[512,128]{1,0:T(8,128)(2,1)} %param.19) | copy-start | bytes 393220
  46.6 104.4 %all-gather.6.cloned.1.call-start = ((), (), s32[]{:S(2)}) async-start(), calls=%async_computation.7 | async-start | bytes 2621440 | tf_op jit(solution)/shard_map/all_gather | solution.py:194
  86.4 33.7 %copy-start.8 = (bf16[128,512]{1,0:T(8,128)(2,1)S(1)}, bf16[128,512]{1,0:T(8,128)(2,1)}, u32[]{:S(2)}) copy-start(bf16[128,512]{1,0:T(8,128)(2,1)} %param.22) | copy-start | bytes 393220
  90.4 3.4 %copy-start.1 = (f32[2,1024,512]{2,1,0:T(8,128)S(1)}, f32[2,1024,512]{2,1,0:T(8,128)}, u32[]{:S(2)}) copy-start(f32[2,1024,512]{2,1,0:T(8,128)} %get-tuple-element.197) | copy-start | bytes 12582916 | tf_op jit(solution)/shard_map/while
  98.8 3.4 %copy-start.1 = (f32[2,1024,512]{2,1,0:T(8,128)S(1)}, f32[2,1024,512]{2,1,0:T(8,128)}, u32[]{:S(2)}) copy-start(f32[2,1024,512]{2,1,0:T(8,128)} %get-tuple-element.197) | copy-start | bytes 12582916 | tf_op jit(solution)/shard_map/while
  107.2 3.4 %copy-start.1 = (f32[2,1024,512]{2,1,0:T(8,128)S(1)}, f32[2,1024,512]{2,1,0:T(8,128)}, u32[]{:S(2)}) copy-start(f32[2,1024,512]{2,1,0:T(8,128)} %get-tuple-element.197) | copy-start | bytes 12582916 | tf_op jit(solution)/shard_map/while
  115.6 3.4 %copy-start.1 = (f32[2,1024,512]{2,1,0:T(8,128)S(1)}, f32[2,1024,512]{2,1,0:T(8,128)}, u32[]{:S(2)}) copy-start(f32[2,1024,512]{2,1,0:T(8,128)} %get-tuple-element.197) | copy-start | bytes 12582916 | tf_op jit(solution)/shard_map/while
  120.0 33.2 %copy-start.2 = (bf16[512,512]{1,0:T(8,128)(2,1)S(1)}, bf16[512,512]{1,0:T(8,128)(2,1)}, u32[]{:S(2)}) copy-start(bf16[512,512]{1,0:T(8,128)(2,1)} %param.15) | copy-start | bytes 1572868
  120.0 33.7 %copy-start.11 = (bf16[512,512]{1,0:T(8,128)(2,1)S(1)}, bf16[512,512]{1,0:T(8,128)(2,1)}, u32[]{:S(2)}) copy-start(bf16[512,512]{1,0:T(8,128)(2,1)} %param.24) | copy-start | bytes 1572868
  120.0 33.7 %copy-start.12 = (f32[512]{0:T(512)S(1)}, f32[512]{0:T(512)}, u32[]{:S(2)}) copy-start(f32[512]{0:T(512)} %param.23) | copy-start | bytes 6148
  121.2 121.4 %reduce-scatter.4.cloned.1.call-start = ((), (), s32[]{:S(2)}) async-start(), calls=%async_computation.4 | async-start | bytes 2359296 | tf_op jit(solution)/shard_map/reduce_scatter | solution.py:231
  153.1 45.7 %copy-start.3 = (bf16[512,512]{1,0:T(8,128)(2,1)}, bf16[512,512]{1,0:T(8,128)(2,1)S(1)}, u32[]{:S(2)}) copy-start(bf16[512,512]{1,0:T(8,128)(2,1)S(1)} %reduce_sum.79) | copy-start | bytes 1572868
  153.1 4.7 %copy-start.9 = (f32[27,512]{1,0:T(8,128)S(1)}, f32[27,512]{1,0:T(8,128)}, u32[]{:S(2)}) copy-start(f32[27,512]{1,0:T(8,128)} %param.25) | copy-start | bytes 165892
  154.3 7.6 %collective-permute-start = (bf16[1,16,16,512]{3,2,1,0:T(8,128)(2,1)S(1)}, bf16[1,16,16,512]{3,2,1,0:T(8,128)(2,1)S(1)}, u32[]{:S(2)}, u32[]{:S(2)}) collective-permute-start(bf16[1,16,16,512]{3,2,1,0:T(8,128)(2,1)S(1)} %bitcast.128), channel_id=1, source_target_pairs={{0,4},{4,8},{8,12},{12,16},{16,20},{20,24},{24,28},{28,32},{32,36}... | collective-permute-start | bytes 786440 | tf_op jit(solution)/shard_map/ppermute | solution.py:28
  156.5 16.3 %collective-permute-start.1 = (bf16[1,16,16,512]{3,2,1,0:T(8,128)(2,1)S(1)}, bf16[1,16,16,512]{3,2,1,0:T(8,128)(2,1)S(1)}, u32[]{:S(2)}, u32[]{:S(2)}) collective-permute-start(bf16[1,16,16,512]{3,2,1,0:T(8,128)(2,1)S(1)} %bitcast.127), channel_id=1, source_target_pairs={{4,0},{8,4},{12,8},{16,12},{20,16},{24,20},{28,24},{32,28},{36,32}... | collective-permute-start | bytes 786440 | tf_op jit(solution)/shard_map/ppermute | solution.py:30
  173.6 4.1 %copy-start.4 = (bf16[512,512]{1,0:T(8,128)(2,1)S(1)}, bf16[512,512]{1,0:T(8,128)(2,1)}, u32[]{:S(2)}) copy-start(bf16[512,512]{1,0:T(8,128)(2,1)} %param.26) | copy-start | bytes 1572868
  178.3 11.9 %collective-permute-start.2 = (bf16[1,16,16,512]{3,2,1,0:T(8,128)(2,1)S(1)}, bf16[1,16,16,512]{3,2,1,0:T(8,128)(2,1)S(1)}, u32[]{:S(2)}, u32[]{:S(2)}) collective-permute-start(bf16[1,16,16,512]{3,2,1,0:T(8,128)(2,1)S(1)} %bitcast.130), channel_id=1, source_target_pairs={{0,4},{4,8},{8,12},{12,16},{16,20},{20,24},{24,28},{28,32},{32,36}... | collective-permute-start | bytes 786440 | tf_op jit(solution)/shard_map/ppermute | solution.py:28
  179.6 14.6 %collective-permute-start.3 = (bf16[1,16,16,512]{3,2,1,0:T(8,128)(2,1)S(1)}, bf16[1,16,16,512]{3,2,1,0:T(8,128)(2,1)S(1)}, u32[]{:S(2)}, u32[]{:S(2)}) collective-permute-start(bf16[1,16,16,512]{3,2,1,0:T(8,128)(2,1)S(1)} %bitcast.129), channel_id=1, source_target_pairs={{4,0},{8,4},{12,8},{16,12},{20,16},{24,20},{28,24},{32,28},{36,32}... | collective-permute-start | bytes 786440 | tf_op jit(solution)/shard_map/ppermute | solution.py:30
  204.8 64.3 %reduce-scatter.6.cloned.1.call-start = ((), (), s32[]{:S(2)}) async-start(), calls=%async_computation.5 | async-start | bytes 327680 | tf_op jit(solution)/shard_map/reduce_scatter | solution.py:231
  242.6 45.4 %reduce-scatter.8.cloned.1.call-start = ((), (), s32[]{:S(2)}) async-start(), calls=%async_computation.6 | async-start | bytes 98304 | tf_op jit(solution)/shard_map/reduce_scatter | solution.py:231
Sparse Core Ops, SparseCore 0:
  46.7 39.6 all-gather.3
  121.3 29.5 all-gather.5
  204.9 37.6 reduce-scatter.3
  244.9 24.1 reduce-scatter.5
  271.5 16.3 reduce-scatter.7
